TPU v7x, 128 devices: a whole 4x4x4 slice. The times are simulated.
128 devices in a mesh: guide: 2 (over core), tensor: 16 (over y, x), batch: 4 (over z).
Axes of the slice: x: 4, y: 4, z: 4, core: 2. Of those that a mesh axis runs over, the one named last changes fastest.
Arguments:
- stream: bfloat16 [2, 512, 2048], P('guide', ('batch', 'tensor')), may hold values from -6 to 6
- attn_gain: float32 [2048], replicated, may hold values from 0.25 to 1.75
- w_qkv: bfloat16 [2048, 3072], P(None, 'tensor'), may hold values from -0.125 to 0.125
- cache_keys: bfloat16 [2, 512, 1024, 512], P('guide', ('batch', 'tensor')), may hold values from -600 to 600
- cache_values: bfloat16 [2, 512, 1024, 512], P('guide', ('batch', 'tensor')), may hold values from -6 to 6
- cache_len: int32 [2, 512], P('guide', ('batch', 'tensor')), may hold values from 1 to 1024, as said below
- w_out: bfloat16 [2048, 2048], P('tensor'), may hold values from -0.125 to 0.125
- mlp_gain: float32 [2048], replicated, may hold values from 0.25 to 1.75
- w_gate: bfloat16 [2048, 8192], P(None, 'tensor'), may hold values from -0.125 to 0.125
- w_up: bfloat16 [2048, 8192], P(None, 'tensor'), may hold values from -0.125 to 0.125
- w_down: bfloat16 [8192, 2048], P('tensor'), may hold values from -0.0625 to 0.0625
- final_gain: float32 [2048], replicated, may hold values from 0.25 to 1.75
- lm_head: bfloat16 [65536, 2048], P(('guide', 'tensor')), may hold values from -128 to 128
- next_gain: float32 [2048], replicated, may hold values from 0.25 to 1.75
- w_next: bfloat16 [2048, 3072], P(None, 'tensor'), may hold values from -0.125 to 0.125
- tenant_counts: int32 [4], replicated, may hold values from 1 to 256, 512 in all
- guide_level: int32 [4], replicated, may hold values from 4 to 16
Outputs:
- logprobs: float32 [512, 65536], P('batch', ('guide', 'tensor'))
- layer_out: bfloat16 [2, 512, 2048], P('guide', ('batch', 'tensor'))
- next_qkv: bfloat16 [2, 512, 3072], P('guide', 'batch', 'tensor')
Inputs may be any that keep to these rules, and one draw needn't show every extreme that they name: `cache_len`: in each branch some request has 1024 cached tokens.
All inputs are finite; a program needn't handle non-finite values.
Results may differ from a plain program's by a relative error of at most 0.024.
Values may be sent and summed in bfloat16 or wider, within the bound.
A program may use at most 128 MiB of HBM per device.

v0:
```python
import math
import jax
import jax.numpy as jnp
from jax import lax
from jax.sharding import PartitionSpec as P

D = 2048
HEADS = 32
KV_HEADS = 8
HEAD_DIM = 64
TENANTS = 4
EPSILON = 1e-05
ROPE_BASE = 500000.0
MASKED = -1e30


def from_partner(block, axis, bit):
    count = lax.axis_size(axis)
    route = []
    for low in range(count):
        high = low | 1 << bit
        if high != low and high < count:
            route += [(low, high), (high, low)]
    return lax.ppermute(block, axis, route)


def rms_norm(values, gain):
    widened = values.astype(jnp.float32)
    factor = lax.rsqrt(jnp.mean(widened * widened, axis=-1, keepdims=True) + EPSILON)
    return (widened * factor * gain).astype(jnp.bfloat16)


def scaled_freq(head_size):
    half_dim = head_size // 2
    steps_up = jnp.arange(half_dim, dtype=jnp.float32)
    base_freq = jnp.exp(steps_up * (-2.0 * math.log(ROPE_BASE) / head_size))
    wavelen = 2.0 * math.pi / base_freq
    smooth = (8192.0 / wavelen - 1.0) / 3.0
    middle = (1.0 - smooth) * base_freq / 32.0 + smooth * base_freq
    return jnp.where(
        wavelen < 2048.0, base_freq, jnp.where(wavelen > 8192.0, base_freq / 32.0, middle)
    )


def rotate(values, position):
    half_dim = values.shape[-1] // 2
    freq = scaled_freq(values.shape[-1])
    angle = position * freq
    cosine = jnp.cos(angle)
    sine = jnp.sin(angle)
    first = values[..., :half_dim].astype(jnp.float32)
    second = values[..., half_dim:].astype(jnp.float32)
    joined = jnp.concatenate(
        [first * cosine - second * sine, second * cosine + first * sine], axis=-1
    )
    return joined.astype(jnp.bfloat16)


def swiglu(normed, w_gate, w_up):
    gate = jnp.dot(normed, w_gate, preferred_element_type=jnp.float32)
    upward = jnp.dot(normed, w_up, preferred_element_type=jnp.float32)
    return (jax.nn.silu(gate) * upward).astype(jnp.bfloat16)


def attend(request_side, keys, values, lengths):
    count = request_side.shape[0]
    kv_width = KV_HEADS * HEAD_DIM
    per_group = HEADS // KV_HEADS
    scale = HEAD_DIM ** (-0.5)
    slot_count = keys.shape[1]
    position = lengths.astype(jnp.float32)[:, None, None]
    queries = rotate(request_side[:, :D].reshape(count, HEADS, HEAD_DIM), position)
    queries = queries.reshape(count, KV_HEADS, per_group, HEAD_DIM)
    new_keys = rotate(
        request_side[:, D : D + kv_width].reshape(count, KV_HEADS, HEAD_DIM), position
    )
    new_values = request_side[:, D + kv_width :].reshape(count, KV_HEADS, HEAD_DIM)
    keys_split = keys.reshape(count, slot_count, KV_HEADS, HEAD_DIM)
    values_split = values.reshape(count, slot_count, KV_HEADS, HEAD_DIM)
    fresh = (
        jnp.einsum("rkgd,rkd->rkg", queries, new_keys, preferred_element_type=jnp.float32) * scale
    )
    slots = jnp.arange(slot_count, dtype=jnp.int32)
    live_mask = (slots[None, :] < lengths[:, None])[:, None, None, :]
    scores = (
        jnp.einsum("rkgd,rlkd->rkgl", queries, keys_split, preferred_element_type=jnp.float32)
        * scale
    )
    scores = jnp.where(live_mask, scores, MASKED)
    peak = jnp.maximum(jnp.max(scores, axis=-1), fresh)
    expd = jnp.where(live_mask, jnp.exp(scores - peak[..., None]), 0.0)
    total = jnp.sum(expd, axis=-1)
    weighted = jnp.einsum(
        "rkgl,rlkd->rkgd",
        expd.astype(jnp.bfloat16),
        values_split,
        preferred_element_type=jnp.float32,
    )
    fresh_exp = jnp.exp(fresh - peak)
    total = total + fresh_exp
    fresh_prob = fresh_exp.astype(jnp.bfloat16).astype(jnp.float32)
    weighted = weighted + fresh_prob[..., None] * new_values.astype(jnp.float32)[:, :, None, :]
    return (weighted / total[..., None]).reshape(count, D).astype(jnp.bfloat16)


def local(
    stream,
    attn_gain,
    w_qkv,
    cache_keys,
    cache_values,
    cache_len,
    w_out,
    mlp_gain,
    w_gate,
    w_up,
    w_down,
    final_gain,
    lm_head,
    next_gain,
    w_next,
    tenant_counts,
    guide_level,
):
    own_rows = stream[0]
    projected = jnp.dot(
        lax.all_gather(rms_norm(own_rows, attn_gain), "tensor", axis=0, tiled=True),
        w_qkv,
        preferred_element_type=jnp.float32,
    ).astype(jnp.bfloat16)
    request_side = lax.all_to_all(projected, "tensor", split_axis=0, concat_axis=1, tiled=True)
    mixed = attend(request_side, cache_keys[0], cache_values[0], cache_len[0])
    head_side = lax.all_to_all(mixed, "tensor", split_axis=1, concat_axis=0, tiled=True)
    selected = head_side
    attn_share = lax.psum_scatter(
        jnp.dot(selected, w_out, preferred_element_type=jnp.float32).astype(jnp.bfloat16),
        "tensor",
        scatter_dimension=0,
        tiled=True,
    ).astype(jnp.float32)
    after_attn = (own_rows.astype(jnp.float32) + attn_share).astype(jnp.bfloat16)
    hidden = swiglu(
        lax.all_gather(rms_norm(after_attn, mlp_gain), "tensor", axis=0, tiled=True), w_gate, w_up
    )
    selected = hidden
    mlp_share = lax.psum_scatter(
        jnp.dot(selected, w_down, preferred_element_type=jnp.float32).astype(jnp.bfloat16),
        "tensor",
        scatter_dimension=0,
        tiled=True,
    ).astype(jnp.float32)
    layer_rows = (after_attn.astype(jnp.float32) + mlp_share).astype(jnp.bfloat16)
    all_out = lax.all_gather(layer_rows, "tensor", axis=0, tiled=True)
    next_rows = jnp.dot(
        rms_norm(all_out, next_gain), w_next, preferred_element_type=jnp.float32
    ).astype(jnp.bfloat16)
    final = rms_norm(all_out, final_gain)
    partner = from_partner(final, "guide", 0)
    is_cond = lax.axis_index("guide") == 0
    cond_rows = jnp.where(is_cond, final, partner)
    uncond_rows = jnp.where(is_cond, partner, final)
    batch_rows = final.shape[0]
    logits = lax.dot_general(
        jnp.concatenate([cond_rows, uncond_rows], axis=0),
        lm_head,
        (((1,), (1,)), ((), ())),
        preferred_element_type=jnp.float32,
    )
    cond_logits = logits[:batch_rows]
    uncond_logits = logits[batch_rows:]
    bounds = jnp.cumsum(tenant_counts)[:-1]
    request_ids = lax.axis_index("batch") * batch_rows + jnp.arange(batch_rows, dtype=jnp.int32)
    tenant = jnp.sum((request_ids[:, None] >= bounds[None, :]).astype(jnp.int32), axis=1)
    chosen = (tenant[:, None] == jnp.arange(TENANTS, dtype=jnp.int32)[None, :]).astype(jnp.float32)
    weight = jnp.sum(chosen * guide_level.astype(jnp.float32)[None, :], axis=1) * 0.25
    guided = uncond_logits + weight[:, None] * (cond_logits - uncond_logits)
    peak = lax.pmax(jnp.max(guided, axis=1), ("guide", "tensor"))
    mass = lax.psum(jnp.sum(jnp.exp(guided - peak[:, None]), axis=1), ("guide", "tensor"))
    logprobs = guided - peak[:, None] - jnp.log(mass)[:, None]
    return (logprobs, layer_rows[None], next_rows[None])


def solution(mesh):
    in_specs = (
        P("guide", ("batch", "tensor"), None),
        P(),
        P(None, "tensor"),
        P("guide", ("batch", "tensor"), None, None),
        P("guide", ("batch", "tensor"), None, None),
        P("guide", ("batch", "tensor")),
        P("tensor", None),
        P(),
        P(None, "tensor"),
        P(None, "tensor"),
        P("tensor", None),
        P(),
        P(("guide", "tensor"), None),
        P(),
        P(None, "tensor"),
        P(),
        P(),
    )
    out_specs = (
        P("batch", ("guide", "tensor")),
        P("guide", ("batch", "tensor"), None),
        P("guide", "batch", "tensor"),
    )
    return jax.shard_map(local, mesh=mesh, in_specs=in_specs, out_specs=out_specs, check_vma=False)
```

profile of v0, /device:TPU:1, one launch (start us, length us, event | category | flops | bytes accessed | tf_op | source)
XLA Modules:
  0.0 462.2 jit_solution(6862168536438569131)
XLA Ops:
  7.2 1.0 fusion.39
  8.2 0.8 fusion.41
  9.1 20.0 %all_gather.9 = bf16[128,2048]{1,0:T(8,128)(2,1)S(1)} all-gather(bf16[8,2048]{1,0:T(8,128)(2,1)S(1)} %fusion.41), channel_id=1, replica_groups=mesh['guide'=2,'tensor'=16,'batch'=4] {'tensor'}, dimensions={0}, use_global_device_ids=true | all-gather | bytes 557056 | tf_op jit(solution)/shard_map/all_gather | solution.py:127
  29.0 1.5 convolution_convert_fusion.3
  30.5 0.7 copy.32
  31.3 4.7 %all-to-all-start = ((bf16[16,8,192]{2,1,0:T(8,128)(2,1)}), bf16[16,8,192]{2,1,0:T(8,128)(2,1)S(1)}, u32[]{:S(2)}, u32[]{:S(2)}) async-start(bf16[16,8,192]{2,1,0:T(8,128)(2,1)} %bitcast.3), calls=%async_computation | async-start | bytes 131072 | tf_op jit(solution)/shard_map/all_to_all | solution.py:131
  36.3 11.4 %copy.34 = bf16[1,8,1024,512]{2,3,1,0:T(8,128)(2,1)} copy(bf16[1,8,1024,512]{3,2,1,0:T(8,128)(2,1)} %param.20) | data formatting | bytes 16777216 | tf_op args[3]
  47.7 11.5 %copy.35 = bf16[1,8,1024,512]{2,3,1,0:T(8,128)(2,1)} copy(bf16[1,8,1024,512]{3,2,1,0:T(8,128)(2,1)} %param.21) | data formatting | bytes 16777216 | tf_op args[4]
  59.8 0.3 fusion.48
  60.1 4.8 %fusion.57 = (f32[8,8,4]{2,1,0:T(8,128)S(1)}, f32[8,8,4,1024]{3,2,1,0:T(4,128)S(1)}) fusion(bf16[8,1024,8,64]{1,3,2,0:T(8,128)(2,1)} %bitcast.42, bf16[8,8,4,32]{3,2,1,0:T(4,128)(2,1)S(1)} %bitcast.47, bf16[8,8,4,32]{3,2,1,0:T(4,128)(2,1)S(1)} %bitcast.45, pred[8,1024]{1,0:T(8,128)(4,1)S(1)} %iota_compare_fusion), kind=kOutput, calls=%fused_computation.103 | convolution fusion | flops 34406144 | bytes 9479168 | tf_op jit(solution)/shard_map/rkgd,rlkd->rkgl/dot_general | solution.py:86
  64.8 0.6 fusion.16
  65.6 5.8 %fusion.5 = bf16[8,8,4,64]{3,2,1,0:T(4,128)(2,1)S(1)} fusion(bf16[8,1024,8,64]{1,3,2,0:T(8,128)(2,1)} %bitcast.43, f32[8,8,4,1024]{3,2,1,0:T(4,128)S(1)} %get-tuple-element.20, f32[8,8,4]{2,1,0:T(8,128)S(1)} %multiply_maximum_fusion, pred[8,1024]{1,0:T(8,128)(4,1)S(1)} %iota_compare_fusion, f32[8,8,4]{2,1,0:T(8,128)S(1)} %get-tuple-element.12, ...), kind=kOutput, calls=%fused_computation.12 | convolution fusion | flops 34406400 | bytes 9497600 | tf_op jit(solution)/shard_map/rkgl,rlkd->rkgd/dot_general | solution.py:93
  71.5 12.9 %all_to_all.35 = bf16[8,16,128]{2,0,1:T(8,128)(2,1)S(1)} all-to-all(bf16[8,16,128]{2,0,1:T(8,128)(2,1)S(1)} %copy.36), channel_id=1, replica_groups=mesh['guide'=2,'tensor'=16,'batch'=4] {'tensor'}, dimensions={1} | all-to-all | bytes 65536 | tf_op jit(solution)/shard_map/all_to_all | solution.py:133
  84.4 2.1 convolution_convert_fusion.1
  86.6 0.6 dynamic-slice
  87.8 88.3 %all-reduce.5.cloned.1.call-done = bf16[128,2048]{1,0:T(8,128)(2,1)} async-done(((bf16[128,2048]{1,0:T(8,128)(2,1)}), bf16[128,2048]{1,0:T(8,128)(2,1)}) %all-reduce.5.cloned.1.call-update) | async-done | bytes 524304
  176.1 0.9 fusion.35
  177.1 17.4 %all_gather.10 = bf16[128,2048]{1,0:T(8,128)(2,1)S(1)} all-gather(bf16[8,2048]{1,0:T(8,128)(2,1)S(1)} %fusion.37), channel_id=1, replica_groups=mesh['guide'=2,'tensor'=16,'batch'=4] {'tensor'}, dimensions={0}, use_global_device_ids=true | all-gather | bytes 557056 | tf_op jit(solution)/shard_map/all_gather | solution.py:143
  194.5 2.0 fusion.58
  196.6 3.2 convolution_convert_fusion
  200.2 89.2 %all-reduce.7.cloned.1.call-done = bf16[128,2048]{1,0:T(8,128)(2,1)} async-done(((bf16[128,2048]{1,0:T(8,128)(2,1)}), bf16[128,2048]{1,0:T(8,128)(2,1)}) %all-reduce.7.cloned.1.call-update) | async-done | bytes 524304
  289.3 0.8 fusion.38
  290.1 17.4 %all_gather.11 = bf16[128,2048]{1,0:T(8,128)(2,1)S(1)} all-gather(bf16[8,2048]{1,0:T(8,128)(2,1)S(1)} %fusion.38), channel_id=1, replica_groups=mesh['guide'=2,'tensor'=16,'batch'=4] {'tensor'}, dimensions={0}, use_global_device_ids=true | all-gather | bytes 557056 | tf_op jit(solution)/shard_map/all_gather | solution.py:153
  307.9 8.1 %collective-permute-start = (bf16[128,2048]{1,0:T(8,128)(2,1)S(1)}, bf16[128,2048]{1,0:T(8,128)(2,1)}, u32[]{:S(2)}, u32[]{:S(2)}) collective-permute-start(bf16[128,2048]{1,0:T(8,128)(2,1)S(1)} %fusion.7), channel_id=1, source_target_pairs={{0,64},{64,0},{1,65},{65,1},{2,66},{66,2},{3,67},{67,3},{4,68},{68... | collective-permute-start | bytes 1572872 | tf_op jit(solution)/shard_map/ppermute | solution.py:24
  316.1 2.2 fusion.6
  318.4 1.4 broadcast_select_fusion.1
  319.8 5.7 %fusion.12 = f32[256,2048]{1,0:T(8,128)S(1)} fusion(bf16[2048,2048]{1,0:T(8,128)(2,1)} %param.29, bf16[128,2048]{1,0:T(8,128)(2,1)S(1)} %get-tuple-element.8, bf16[128,2048]{1,0:T(8,128)(2,1)S(1)} %get-tuple-element.7), kind=kOutput, calls=%fused_computation.22 | convolution fusion | flops 2149580800 | bytes 11534336 | tf_op jit(solution)/shard_map/dot_general | solution.py:163
  325.5 0.4 fusion.54
  326.0 65.0 %pmax.7 = f32[128]{0:T(128)S(1)} all-reduce(f32[128]{0:T(128)S(1)} %get-tuple-element.3), channel_id=1, replica_groups=mesh['guide'=2,'tensor'=16,'batch'=4] {'guide','tensor'}, use_global_device_ids=true, to_apply=%region_11.12 | all-reduce | flops 128 | bytes 1024 | tf_op jit(solution)/shard_map/pmax | solution.py:177
  391.0 0.3 exponential_reduce_fusion
  391.3 62.9 %psum.7 = f32[128]{0:T(128)S(1)} all-reduce(f32[128]{0:T(128)S(1)} %exponential_reduce_fusion), channel_id=1, replica_groups=mesh['guide'=2,'tensor'=16,'batch'=4] {'guide','tensor'}, use_global_device_ids=true, to_apply=%region_13.14 | all-reduce | flops 128 | bytes 1024 | tf_op jit(solution)/shard_map/psum | solution.py:178
  454.2 1.1 subtract_subtract_fusion
  (58 shorter events, 2.1 us)
Async XLA Ops:
  7.2 189.4 %copy-start = (bf16[512,2048]{1,0:T(8,128)(2,1)S(1)}, bf16[512,2048]{1,0:T(8,128)(2,1)}, u32[]{:S(2)}) copy-start(bf16[512,2048]{1,0:T(8,128)(2,1)} %param.27) | copy-start | bytes 6291460
  7.2 28.9 %copy-start.5 = (s32[1,8]{1,0:T(1,128)S(1)}, s32[1,8]{1,0:T(1,128)}, u32[]{:S(2)}) copy-start(s32[1,8]{1,0:T(1,128)} %param.22) | copy-start | bytes 100
  31.3 27.9 %all-to-all-start = ((bf16[16,8,192]{2,1,0:T(8,128)(2,1)}), bf16[16,8,192]{2,1,0:T(8,128)(2,1)S(1)}, u32[]{:S(2)}, u32[]{:S(2)}) async-start(bf16[16,8,192]{2,1,0:T(8,128)(2,1)} %bitcast.3), calls=%async_computation | async-start | bytes 131072 | tf_op jit(solution)/shard_map/all_to_all | solution.py:131
  36.0 140.2 %all-reduce.5.cloned.1.call-start = ((), (), s32[]{:S(2)}) async-start(), calls=%async_computation.2 | async-start | bytes 1048576
  65.5 21.1 %copy-start.9 = (u32[128]{0:T(128)S(1)}, u32[128]{0:T(128)}, u32[]{:S(2)}) copy-start(u32[128]{0:T(128)} %constant.67) | copy-start | bytes 1540
  65.5 110.6 %copy-start.1 = (bf16[1,8,2048]{2,1,0:T(8,128)(2,1)S(1)}, bf16[1,8,2048]{2,1,0:T(8,128)(2,1)}, u32[]{:S(2)}) copy-start(bf16[1,8,2048]{2,1,0:T(8,128)(2,1)} %param.17) | copy-start | bytes 98308
  65.6 111.5 %copy-start.4 = (f32[2048]{0:T(1024)S(1)}, f32[2048]{0:T(1024)}, u32[]{:S(2)}) copy-start(f32[2048]{0:T(1024)} %param.24) | copy-start | bytes 24580
  86.5 202.8 %all-reduce.7.cloned.1.call-start = ((), (), s32[]{:S(2)}) async-start(), calls=%async_computation.3 | async-start | bytes 1048576
  196.6 3.3 copy-start.7
  196.6 111.1 %copy-start.3 = (f32[2048]{0:T(1024)S(1)}, f32[2048]{0:T(1024)}, u32[]{:S(2)}) copy-start(f32[2048]{0:T(1024)} %param.28) | copy-start | bytes 24580
  199.8 116.2 %copy-start.8 = (s32[4]{0:T(128)S(1)}, s32[4]{0:T(128)}, u32[]{:S(2)}) copy-start(s32[4]{0:T(128)} %param.33) | copy-start | bytes 52
  199.8 116.3 %copy-start.6 = (f32[2048]{0:T(1024)S(1)}, f32[2048]{0:T(1024)}, u32[]{:S(2)}) copy-start(f32[2048]{0:T(1024)} %param.30) | copy-start | bytes 24580
  290.1 29.7 %copy-start.2 = (bf16[8,2048]{1,0:T(8,128)(2,1)}, bf16[8,2048]{1,0:T(8,128)(2,1)S(1)}, u32[]{:S(2)}) copy-start(bf16[8,2048]{1,0:T(8,128)(2,1)S(1)} %fusion.38) | copy-start | bytes 98308
  307.9 10.4 %collective-permute-start = (bf16[128,2048]{1,0:T(8,128)(2,1)S(1)}, bf16[128,2048]{1,0:T(8,128)(2,1)}, u32[]{:S(2)}, u32[]{:S(2)}) collective-permute-start(bf16[128,2048]{1,0:T(8,128)(2,1)S(1)} %fusion.7), channel_id=1, source_target_pairs={{0,64},{64,0},{1,65},{65,1},{2,66},{66,2},{3,67},{67,3},{4,68},{68... | collective-permute-start | bytes 1572872 | tf_op jit(solution)/shard_map/ppermute | solution.py:24
Sparse Core Ops, SparseCore 0:
  86.7 89.4 all-reduce.4
  200.0 89.2 all-reduce.6
where the time goes:
time: 464 us; the launch traced here: 462 us
  blocking collectives  196 us (42%)
  waiting for transfers between devices  178 us (38%)
  matrix products  27.7 us (6%)
  local copies, waits for them, and re-layouts  24.8 us (5%)
  between operations  14.9 us (3%)
  starting transfers between devices  12.9 us (3%)
  other arithmetic  8.77 us (2%)
    unnamed x4, waiting for transfers between devices  177 us
    pmax x1, blocking collectives, local(): peak = lax.pmax(jnp.max(guided, axis=1), ('guide', 'tensor'))  65 us
    psum x1, blocking collectives, local(): lax.psum(jnp.sum(jnp.exp(guided - peak[:, None]), axis=1), ('guide', 'ten...  62.9 us
    unnamed x23, local copies, waits for them, and re-layouts  23.5 us
    all_gather x1, blocking collectives, local(): lax.all_gather(rms_norm(own_rows, attn_gain), 'tensor', axis=0, tiled=True)  20 us
    all_gather x1, blocking collectives, local(): all_out = lax.all_gather(layer_rows, 'tensor', axis=0, tiled=True)  17.4 us
    all_gather x1, blocking collectives, local(): lax.all_gather(rms_norm(after_attn, mlp_gain), 'tensor', axis=0, tiled=True)  17.4 us
    all_to_all x1, blocking collectives, local(): lax.all_to_all(mixed, 'tensor', split_axis=1, concat_axis=0, tiled=True)  12.9 us
  transfers between devices with their start and end apart: 4, of which 2 were waited for; matrix products, arithmetic and copies ran while one was open for 6% of the time, Pallas kernels for 0%

commit v1 on v0

--- a/solution.py
+++ b/solution.py
@@ -3,6 +3,7 @@
 import jax.numpy as jnp
 from jax import lax
 from jax.sharding import PartitionSpec as P
+from jax.lax import all_to_all, axis_size
 
 D = 2048
 HEADS = 32
@@ -150,7 +151,9 @@
         tiled=True,
     ).astype(jnp.float32)
     layer_rows = (after_attn.astype(jnp.float32) + mlp_share).astype(jnp.bfloat16)
-    all_out = lax.all_gather(layer_rows, "tensor", axis=0, tiled=True)
+    all_out = jnp.concatenate(
+        all_to_all(jnp.stack(axis_size("tensor") * [layer_rows], 0), "tensor", 0, 0), 0
+    )
     next_rows = jnp.dot(
         rms_norm(all_out, next_gain), w_next, preferred_element_type=jnp.float32
     ).astype(jnp.bfloat16)

time: 464 us -> 456 us (0.983)
  blocking collectives: 196 us -> 178 us
  waiting for transfers between devices: 178 us -> 187 us
    all_gather x1 -> x0, blocking collectives: 17.4 us -> none  [local(): all_out = lax.all_gather(layer_rows, 'tensor', axis=0, tiled=True)]
    all_to_all x0 -> x1, waiting for transfers between devices: none -> 8.71 us  [local(): all_to_all(jnp.stack(axis_size('tensor') * [layer_rows], 0), 'tensor', 0, 0)]
  transfers between devices with their start and end apart: 4 -> 5, of which waited for: 2 -> 3; matrix products, arithmetic and copies ran while one was open for 6% -> 6% of each run, Pallas kernels for 0% -> 0%
where the time goes in v1:
time: 456 us; the launch traced here: 455 us
  waiting for transfers between devices  187 us (41%)
  blocking collectives  178 us (39%)
  matrix products  27.6 us (6%)
  local copies, waits for them, and re-layouts  25.8 us (6%)
  between operations  14.9 us (3%)
  starting transfers between devices  13.1 us (3%)
  other arithmetic  8.77 us (2%)
    unnamed x4, waiting for transfers between devices  178 us
    psum x1, blocking collectives, local(): lax.psum(jnp.sum(jnp.exp(guided - peak[:, None]), axis=1), ('guide', 'ten...  64.5 us
    pmax x1, blocking collectives, local(): peak = lax.pmax(jnp.max(guided, axis=1), ('guide', 'tensor'))  63.5 us
    unnamed x23, local copies, waits for them, and re-layouts  23.5 us
    all_gather x1, blocking collectives, local(): lax.all_gather(rms_norm(own_rows, attn_gain), 'tensor', axis=0, tiled=True)  20 us
    all_gather x1, blocking collectives, local(): lax.all_gather(rms_norm(after_attn, mlp_gain), 'tensor', axis=0, tiled=True)  17.4 us
    all_to_all x1, blocking collectives, local(): lax.all_to_all(mixed, 'tensor', split_axis=1, concat_axis=0, tiled=True)  12.9 us
  transfers between devices with their start and end apart: 5, of which 3 were waited for; matrix products, arithmetic and copies ran while one was open for 6% of the time, Pallas kernels for 0%

profile of v1, /device:TPU:1, one launch (start us, length us, event | category | flops | bytes accessed | tf_op | source)
XLA Modules:
  0.0 455.0 jit_solution(14989265230573051497)
XLA Ops:
  7.2 1.0 fusion.40
  8.2 0.8 fusion.42
  9.1 20.0 %all_gather.6 = bf16[128,2048]{1,0:T(8,128)(2,1)S(1)} all-gather(bf16[8,2048]{1,0:T(8,128)(2,1)S(1)} %fusion.42), channel_id=1, replica_groups=mesh['guide'=2,'tensor'=16,'batch'=4] {'tensor'}, dimensions={0}, use_global_device_ids=true | all-gather | bytes 557056 | tf_op jit(solution)/shard_map/all_gather | solution.py:128
  29.0 1.5 convolution_convert_fusion.3
  30.5 0.7 copy.32
  31.3 4.7 %all-to-all-start = ((bf16[16,8,192]{2,1,0:T(8,128)(2,1)}), bf16[16,8,192]{2,1,0:T(8,128)(2,1)S(1)}, u32[]{:S(2)}, u32[]{:S(2)}) async-start(bf16[16,8,192]{2,1,0:T(8,128)(2,1)} %bitcast.3), calls=%async_computation | async-start | bytes 131072 | tf_op jit(solution)/shard_map/all_to_all | solution.py:132
  36.3 11.4 %copy.34 = bf16[1,8,1024,512]{2,3,1,0:T(8,128)(2,1)} copy(bf16[1,8,1024,512]{3,2,1,0:T(8,128)(2,1)} %param.20) | data formatting | bytes 16777216 | tf_op args[3]
  47.7 11.5 %copy.35 = bf16[1,8,1024,512]{2,3,1,0:T(8,128)(2,1)} copy(bf16[1,8,1024,512]{3,2,1,0:T(8,128)(2,1)} %param.21) | data formatting | bytes 16777216 | tf_op args[4]
  60.1 4.8 %fusion.58 = (f32[8,8,4]{2,1,0:T(8,128)S(1)}, f32[8,8,4,1024]{3,2,1,0:T(4,128)S(1)}) fusion(bf16[8,1024,8,64]{1,3,2,0:T(8,128)(2,1)} %bitcast.57, bf16[8,8,4,32]{3,2,1,0:T(4,128)(2,1)S(1)} %bitcast.62, bf16[8,8,4,32]{3,2,1,0:T(4,128)(2,1)S(1)} %bitcast.60, pred[8,1024]{1,0:T(8,128)(4,1)S(1)} %iota_compare_fusion), kind=kOutput, calls=%fused_computation.104 | convolution fusion | flops 34406144 | bytes 9479168 | tf_op jit(solution)/shard_map/rkgd,rlkd->rkgl/dot_general | solution.py:87
  64.8 0.6 fusion.17
  65.6 5.8 %fusion.3 = bf16[8,8,4,64]{3,2,1,0:T(4,128)(2,1)S(1)} fusion(bf16[8,1024,8,64]{1,3,2,0:T(8,128)(2,1)} %bitcast.58, f32[8,8,4,1024]{3,2,1,0:T(4,128)S(1)} %get-tuple-element.20, f32[8,8,4]{2,1,0:T(8,128)S(1)} %multiply_maximum_fusion, pred[8,1024]{1,0:T(8,128)(4,1)S(1)} %iota_compare_fusion, f32[8,8,4]{2,1,0:T(8,128)S(1)} %get-tuple-element.12, ...), kind=kOutput, calls=%fused_computation.10 | convolution fusion | flops 34406400 | bytes 9497600 | tf_op jit(solution)/shard_map/rkgl,rlkd->rkgd/dot_general | solution.py:94
  71.5 12.9 %all_to_all.40 = bf16[8,16,128]{2,0,1:T(8,128)(2,1)S(1)} all-to-all(bf16[8,16,128]{2,0,1:T(8,128)(2,1)S(1)} %copy.36), channel_id=1, replica_groups=mesh['guide'=2,'tensor'=16,'batch'=4] {'tensor'}, dimensions={1} | all-to-all | bytes 65536 | tf_op jit(solution)/shard_map/all_to_all | solution.py:134
  84.4 2.1 convolution_convert_fusion.1
  86.6 0.6 dynamic-slice
  87.8 88.3 %all-reduce.5.cloned.1.call-done = bf16[128,2048]{1,0:T(8,128)(2,1)} async-done(((bf16[128,2048]{1,0:T(8,128)(2,1)}), bf16[128,2048]{1,0:T(8,128)(2,1)}) %all-reduce.5.cloned.1.call-update) | async-done | bytes 524304
  176.1 0.9 fusion.36
  177.1 17.4 %all_gather.7 = bf16[128,2048]{1,0:T(8,128)(2,1)S(1)} all-gather(bf16[8,2048]{1,0:T(8,128)(2,1)S(1)} %fusion.38), channel_id=1, replica_groups=mesh['guide'=2,'tensor'=16,'batch'=4] {'tensor'}, dimensions={0}, use_global_device_ids=true | all-gather | bytes 557056 | tf_op jit(solution)/shard_map/all_gather | solution.py:144
  194.5 2.0 fusion.59
  196.6 3.2 convolution_convert_fusion
  199.8 89.5 %all-reduce.7.cloned.1.call-done = bf16[128,2048]{1,0:T(8,128)(2,1)} async-done(((bf16[128,2048]{1,0:T(8,128)(2,1)}), bf16[128,2048]{1,0:T(8,128)(2,1)}) %all-reduce.7.cloned.1.call-update) | async-done | bytes 524304
  289.3 0.8 fusion.39
  290.1 0.8 stack.4
  291.0 4.1 all-to-all-start.2
  295.3 8.7 %all-to-all-done.2 = bf16[16,8,2048]{2,1,0:T(8,128)(2,1)S(1)} async-done(((bf16[16,8,2048]{2,1,0:T(8,128)(2,1)}), bf16[16,8,2048]{2,1,0:T(8,128)(2,1)S(1)}, u32[]{:S(2)}, u32[]{:S(2)}) %all-to-all-start.2) | async-done | bytes 524320 | tf_op jit(solution)/shard_map/all_to_all | solution.py:155
  304.5 4.2 collective-permute-start
  308.9 2.2 fusion.4
  311.1 1.4 broadcast_select_fusion.1
  312.5 5.7 %fusion.13 = f32[256,2048]{1,0:T(8,128)S(1)} fusion(bf16[2048,2048]{1,0:T(8,128)(2,1)} %param.29, bf16[128,2048]{1,0:T(8,128)(2,1)S(1)} %get-tuple-element.8, bf16[128,2048]{1,0:T(8,128)(2,1)S(1)} %get-tuple-element.7), kind=kOutput, calls=%fused_computation.23 | convolution fusion | flops 2149580800 | bytes 11534336 | tf_op jit(solution)/shard_map/dot_general | solution.py:166
  318.3 0.4 fusion.55
  318.7 63.5 %pmax.7 = f32[128]{0:T(128)S(1)} all-reduce(f32[128]{0:T(128)S(1)} %get-tuple-element.3), channel_id=1, replica_groups=mesh['guide'=2,'tensor'=16,'batch'=4] {'guide','tensor'}, use_global_device_ids=true, to_apply=%region_11.12 | all-reduce | flops 128 | bytes 1024 | tf_op jit(solution)/shard_map/pmax | solution.py:180
  382.5 64.5 %psum.7 = f32[128]{0:T(128)S(1)} all-reduce(f32[128]{0:T(128)S(1)} %exponential_reduce_fusion), channel_id=1, replica_groups=mesh['guide'=2,'tensor'=16,'batch'=4] {'guide','tensor'}, use_global_device_ids=true, to_apply=%region_13.14 | all-reduce | flops 128 | bytes 1024 | tf_op jit(solution)/shard_map/psum | solution.py:181
  447.0 1.1 subtract_subtract_fusion
  (61 shorter events, 2.7 us)
Async XLA Ops:
  7.2 189.4 %copy-start = (bf16[512,2048]{1,0:T(8,128)(2,1)S(1)}, bf16[512,2048]{1,0:T(8,128)(2,1)}, u32[]{:S(2)}) copy-start(bf16[512,2048]{1,0:T(8,128)(2,1)} %param.27) | copy-start | bytes 6291460
  7.2 28.9 %copy-start.5 = (s32[1,8]{1,0:T(1,128)S(1)}, s32[1,8]{1,0:T(1,128)}, u32[]{:S(2)}) copy-start(s32[1,8]{1,0:T(1,128)} %param.22) | copy-start | bytes 100
  31.3 27.9 %all-to-all-start = ((bf16[16,8,192]{2,1,0:T(8,128)(2,1)}), bf16[16,8,192]{2,1,0:T(8,128)(2,1)S(1)}, u32[]{:S(2)}, u32[]{:S(2)}) async-start(bf16[16,8,192]{2,1,0:T(8,128)(2,1)} %bitcast.3), calls=%async_computation | async-start | bytes 131072 | tf_op jit(solution)/shard_map/all_to_all | solution.py:132
  36.0 140.2 %all-reduce.5.cloned.1.call-start = ((), (), s32[]{:S(2)}) async-start(), calls=%async_computation.3 | async-start | bytes 1048576
  65.5 21.1 %copy-start.9 = (u32[128]{0:T(128)S(1)}, u32[128]{0:T(128)}, u32[]{:S(2)}) copy-start(u32[128]{0:T(128)} %constant.67) | copy-start | bytes 1540
  65.5 110.6 %copy-start.1 = (bf16[1,8,2048]{2,1,0:T(8,128)(2,1)S(1)}, bf16[1,8,2048]{2,1,0:T(8,128)(2,1)}, u32[]{:S(2)}) copy-start(bf16[1,8,2048]{2,1,0:T(8,128)(2,1)} %param.17) | copy-start | bytes 98308
  65.6 111.5 %copy-start.4 = (f32[2048]{0:T(1024)S(1)}, f32[2048]{0:T(1024)}, u32[]{:S(2)}) copy-start(f32[2048]{0:T(1024)} %param.24) | copy-start | bytes 24580
  86.5 202.8 %all-reduce.7.cloned.1.call-start = ((), (), s32[]{:S(2)}) async-start(), calls=%async_computation.4 | async-start | bytes 1048576
  199.8 95.3 %copy-start.7 = (s32[4]{0:T(128)S(1)}, s32[4]{0:T(128)}, u32[]{:S(2)}) copy-start(s32[4]{0:T(128)} %param.32) | copy-start | bytes 52
  199.8 104.5 %copy-start.3 = (f32[2048]{0:T(1024)S(1)}, f32[2048]{0:T(1024)}, u32[]{:S(2)}) copy-start(f32[2048]{0:T(1024)} %param.28) | copy-start | bytes 24580
  199.8 109.0 %copy-start.8 = (s32[4]{0:T(128)S(1)}, s32[4]{0:T(128)}, u32[]{:S(2)}) copy-start(s32[4]{0:T(128)} %param.33) | copy-start | bytes 52
  199.8 109.1 %copy-start.6 = (f32[2048]{0:T(1024)S(1)}, f32[2048]{0:T(1024)}, u32[]{:S(2)}) copy-start(f32[2048]{0:T(1024)} %param.30) | copy-start | bytes 24580
  290.1 21.0 %copy-start.2 = (bf16[8,2048]{1,0:T(8,128)(2,1)}, bf16[8,2048]{1,0:T(8,128)(2,1)S(1)}, u32[]{:S(2)}) copy-start(bf16[8,2048]{1,0:T(8,128)(2,1)S(1)} %fusion.39) | copy-start | bytes 98308
  291.0 13.1 %all-to-all-start.2 = ((bf16[16,8,2048]{2,1,0:T(8,128)(2,1)}), bf16[16,8,2048]{2,1,0:T(8,128)(2,1)S(1)}, u32[]{:S(2)}, u32[]{:S(2)}) async-start(bf16[16,8,2048]{2,1,0:T(8,128)(2,1)} %stack.4), calls=%async_computation.2 | async-start | bytes 1048576 | tf_op jit(solution)/shard_map/all_to_all | solution.py:155
  304.5 6.6 %collective-permute-start = (bf16[128,2048]{1,0:T(8,128)(2,1)S(1)}, bf16[128,2048]{1,0:T(8,128)(2,1)}, u32[]{:S(2)}, u32[]{:S(2)}) collective-permute-start(bf16[128,2048]{1,0:T(8,128)(2,1)S(1)} %fusion.8), channel_id=1, source_target_pairs={{0,64},{64,0},{1,65},{65,1},{2,66},{66,2},{3,67},{67,3},{4,68},{68... | collective-permute-start | bytes 1572872 | tf_op jit(solution)/shard_map/ppermute | solution.py:25
Sparse Core Ops, SparseCore 0:
  86.7 89.4 all-reduce.4
  200.0 89.3 all-reduce.6
